TPU v7x, 256 devices: a whole 4x4x8 slice. The times are simulated.
256 devices in a mesh: rcv: 4 (over y_lo, core), slab: 64 (over z, y_hi, x).
Axes of the slice: x: 4, y: 4 (y_hi: 2, y_lo: 2; y = y_hi * 2 + y_lo), z: 8, core: 2. Of those that a mesh axis runs over, the one named last changes fastest.
Arguments:
- displacement: bfloat16 [2, 16, 3, 128, 16, 1024], P(None, None, None, 'slab'), may hold values from -6 to 6
- green: bfloat16 [8, 16, 6, 128, 16, 1024], P('rcv', None, None, 'slab'), may hold values from -0.1796875 to 0.1796875
- lame_lambda: float32 [128, 16, 1024], P('slab'), may hold values from 0.5 to 2
- shear_modulus: float32 [128, 16, 1024], P('slab'), may hold values from 0.3 to 1.5
- filters: float32 [2, 8, 9], P(None, 'rcv'), may hold values from -2 to 2
- pairs: int32 [2, 8], P(None, 'rcv'), may hold values 0 or 1
Outputs:
- kernels: float32 [2, 128, 16, 1024], P(None, 'slab', 'rcv')
Inputs may be any that keep to these rules, and one draw needn't show every extreme that they name: `pairs`: 1 marks a pair that is used, 0 one that is not.
All inputs are finite; a program needn't handle non-finite values. No bound on the sum of `pairs` on one device may be relied on, other than what follows from the above.
Results may differ from a plain program's by a relative error of at most 0.0029.
Values may be sent and summed in bfloat16 or wider, within the bound.
A program may use at most 192 MiB of HBM per device.

v0:
```python
import jax
import jax.numpy as jnp
from jax import lax
from jax.sharding import PartitionSpec as P


def padded_2(array, sides, width):
    for axis, dim in sides:
        devices, length = (lax.axis_size(axis), array.shape[dim])
        up = [(i, (i + 1) % devices) for i in range(devices - 1)]
        down = [(j, i) for i, j in up]
        last = lax.slice_in_dim(array, length - width, length, axis=dim)
        initial = lax.slice_in_dim(array, 0, width, axis=dim)
        before = lax.ppermute(last, axis, up)
        after = lax.ppermute(initial, axis, down)
        array = jnp.concatenate([before, array, after], axis=dim)
    return array


def derivative(field, axis):
    length = field.shape[axis]
    pad_width = [(0, 0)] * field.ndim
    pad_width[axis] = (2, 2)
    padded = jnp.pad(field, pad_width)

    def window(offset):
        return lax.slice_in_dim(padded, 2 + offset, 2 + offset + length, axis=axis)

    return (8.0 * (window(1) - window(-1)) - (window(2) - window(-2))) / 12.0


def depth_derivative(extended, length):

    def window(offset):
        return lax.slice_in_dim(extended, 2 + offset, 2 + offset + length, axis=3)

    return (8.0 * (window(1) - window(-1)) - (window(2) - window(-2))) / 12.0


def compose(along_cols, along_rows, along_depth, lame_lambda, shear_modulus):
    strain_xx = along_cols[:, :, 0]
    strain_yy = along_rows[:, :, 1]
    strain_zz = along_depth[:, :, 2]
    strain_yz = 0.5 * (along_depth[:, :, 1] + along_rows[:, :, 2])
    strain_xz = 0.5 * (along_depth[:, :, 0] + along_cols[:, :, 2])
    strain_xy = 0.5 * (along_rows[:, :, 0] + along_cols[:, :, 1])
    strain_trace = strain_xx + strain_yy + strain_zz
    volume_term = lame_lambda * strain_trace
    double_shear = 2.0 * shear_modulus
    components = [
        volume_term + double_shear * strain_xx,
        volume_term + double_shear * strain_yy,
        volume_term + double_shear * strain_zz,
        double_shear * strain_yz,
        double_shear * strain_xz,
        double_shear * strain_xy,
    ]
    return jnp.stack(components, axis=2).astype(jnp.bfloat16)


def contribution(stress_one, filter_taps, green_one):
    lag_total = filter_taps.shape[0]
    half_lags = lag_total // 2
    snap_count = stress_one.shape[0]
    padded = jnp.pad(stress_one, [(half_lags, half_lags)] + [(0, 0)] * (stress_one.ndim - 1))
    filtered = jnp.zeros(stress_one.shape, jnp.float32)
    for lag_index in range(lag_total):
        filtered = filtered + filter_taps[lag_index] * padded[
            lag_index : lag_index + snap_count
        ].astype(jnp.float32)
    weights = jnp.array([1.0, 1.0, 1.0, 2.0, 2.0, 2.0], jnp.float32).reshape(1, 6, 1, 1, 1)
    return jnp.sum(filtered * green_one.astype(jnp.float32) * weights, axis=(0, 1))


def on_device(displacement, green, lame_lambda, shear_modulus, filters, pairs):
    sources, snap_count, components, planes, row_count, col_count = displacement.shape
    extended = padded_2(displacement, (("slab", 3),), 2)
    field = extended.astype(jnp.float32)
    interior = field[:, :, :, 2 : planes + 2]
    along_depth = depth_derivative(field, planes)
    along_rows = derivative(interior, 4)
    along_cols = derivative(interior, 5)
    stress = compose(along_cols, along_rows, along_depth, lame_lambda, shear_modulus)
    station_count = green.shape[0]
    slots = sources * station_count
    flat_pairs = pairs.reshape(-1)
    initial = jnp.zeros((sources, planes, row_count, col_count), jnp.float32)

    def add_slot(slot, kernel_acc, weight):
        source = slot // station_count
        station = slot % station_count
        stress_one = lax.dynamic_index_in_dim(stress, source, 0, keepdims=False)
        green_one = lax.dynamic_index_in_dim(green, station, 0, keepdims=False)
        filter_taps = filters[source, station]
        term = weight * contribution(stress_one, filter_taps, green_one)
        current = lax.dynamic_index_in_dim(kernel_acc, source, 0, keepdims=False)
        return lax.dynamic_update_index_in_dim(kernel_acc, current + term, source, 0)

    def add_masked(slot, kernel_acc):
        return add_slot(slot, kernel_acc, flat_pairs[slot].astype(jnp.float32))

    kernel_acc = lax.fori_loop(0, slots, add_masked, initial)
    return lax.psum_scatter(kernel_acc, "rcv", scatter_dimension=2, tiled=True)


def solution(mesh):
    placed = (
        P(None, None, None, "slab", None, None),
        P("rcv", None, None, "slab", None, None),
        P("slab", None, None),
        P("slab", None, None),
        P(None, "rcv", None),
        P(None, "rcv"),
    )
    return jax.shard_map(
        on_device,
        mesh=mesh,
        in_specs=placed,
        out_specs=P(None, "slab", "rcv", None),
        check_vma=False,
    )
```

profile of v0, /device:TPU:161, one launch (start us, length us, event | category | flops | bytes accessed | tf_op | source)
XLA Modules:
  0.0 492.6 jit_solution(11345567811565906085)
XLA Ops:
  6.5 3.1 collective-permute-start
  9.7 6.7 %collective-permute-start.1 = (bf16[2,16,3,2,16,1024]{5,4,3,2,1,0:T(8,128)(2,1)}, bf16[2,16,3,2,16,1024]{5,4,3,2,1,0:T(8,128)(2,1)}, u32[]{:S(2)}, u32[]{:S(2)}) collective-permute-start(bf16[2,16,3,2,16,1024]{5,4,3,2,1,0:T(8,128)(2,1)} %param.9), channel_id=1, source_target_pairs={{1,0},{2,1},{3,2},{4,3},{5,4},{6,5},{7,6},{8,7},{9,8},{10,9},{11,1... | collective-permute-start | bytes 18874376 | tf_op jit(solution)/shard_map/ppermute | solution.py:15
  16.3 0.8 reshape.44
  17.1 0.9 broadcast_multiply_fusion
  18.0 131.6 %collective-permute-done = bf16[2,16,3,2,16,1024]{5,4,3,2,1,0:T(8,128)(2,1)} collective-permute-done((bf16[2,16,3,2,16,1024]{5,4,3,2,1,0:T(8,128)(2,1)}, bf16[2,16,3,2,16,1024]{5,4,3,2,1,0:T(8,128)(2,1)}, u32[]{:S(2)}, u32[]{:S(2)}) %collective-permute-start) | collective-permute-done | bytes 6291488 | tf_op jit(solution)/shard_map/ppermute | solution.py:14
  149.6 0.9 collective-permute-done.1
  150.5 20.2 %maximum_convert_fusion = f32[2,16,3,6,16,1024]{5,4,3,2,1,0:T(8,128)} fusion(bf16[2,16,3,2,16,1024]{5,4,3,2,1,0:T(8,128)(2,1)} %collective-permute-done.1, bf16[2,16,3,2,16,1024]{5,4,3,2,1,0:T(8,128)(2,1)} %param.9, bf16[2,16,3,2,16,1024]{5,4,3,2,1,0:T(8,128)(2,1)} %collective-permute-done), kind=kLoop, calls=%fused_computation.19 | loop fusion | flops 28311552 | bytes 56623104 | tf_op jit(solution)/shard_map/convert_element_type | solution.py:78
  170.7 31.8 %fusion.14 = (f32[2,16,3,2,16,1024]{5,4,3,2,1,0:T(8,128)}, f32[2,16,3,2,16,1024]{5,4,3,2,1,0:T(8,128)}) fusion(f32[2,16,3,6,16,1024]{5,4,3,2,1,0:T(8,128)} %maximum_convert_fusion), kind=kLoop, calls=%fused_computation.36 | loop fusion | flops 15728640 | bytes 88080384 | tf_op jit(solution)/shard_map/div | solution.py:37
  202.5 43.5 %fusion.11 = (f32[2,16,3,2,16,1024]{5,4,3,2,1,0:T(8,128)}, f32[2,16,3,2,16,1024]{5,4,3,2,1,0:T(8,128)}) fusion(f32[2,16,3,2,16,1024]{5,4,3,2,1,0:T(8,128)} %get-tuple-element.231), kind=kLoop, calls=%fused_computation.32 | loop fusion | flops 31457280 | bytes 37748736 | tf_op jit(solution)/shard_map/div | solution.py:29
  246.1 6.4 %fusion.22 = (bf16[2,16,6,2,16,1024]{5,4,3,2,1,0:T(8,128)(2,1)S(1)}, f32[2,16,1,2,16,1024]{5,4,3,2,1,0:T(8,128)S(1)}) fusion(f32[2,16,3,2,16,1024]{5,4,3,2,1,0:T(8,128)} %get-tuple-element.233, f32[2,16,1024]{2,1,0:T(8,128)S(1)} %broadcast_multiply_fusion, f32[2,16,3,2,16,1024]{5,4,3,2,1,0:T(8,128)} %get-tuple-element.230, ...), kind=kLoop, calls=%fused_computation.52 | loop fusion | flops 6291455 | bytes 19136512
  252.4 0.0 copy-start.2
  252.4 0.0 slice-start
  252.4 3.5 fusion.23
  255.9 0.0 slice-start.1
  255.9 3.5 fusion.24
  259.4 0.0 slice-start.2
  259.4 4.7 fusion.25
  264.2 0.0 copy-start.4
  264.2 3.3 fusion.26
  267.5 3.3 fusion.27
  270.8 4.5 copy-done
  275.3 0.0 copy-done.4
  275.3 161.6 %while.16 = (s32[]{:T(128)}, f32[2,2,16,1024]{3,2,1,0:T(8,128)S(1)}, s32[4]{0:T(128)S(1)}, f32[2,2,9]{2,1,0:T(2,128)}, bf16[2,16,6,2,16,1024]{5,4,3,2,1,0:T(8,12...) while((s32[]{:T(128)}, ...), condition=%wide.region_2.3_spmd.clone, body=%wide.region_0.2_spmd.sunk.clone.sunk | while | flops 94404624 | bytes 25690652 | solution.py:102
  275.3 6.8 %dynamic-slice_bitcast_fusion.2 = bf16[16,6,2,16,1024]{4,3,2,1,0:T(8,128)(2,1)} fusion(bf16[2,16,6,2,16,1024]{5,4,3,2,1,0:T(8,128)(2,1)} %get-tuple-element.315, s32[]{:T(128)S(6)} %select_n.80), kind=kLoop, calls=%fused_computation.11.clone.1 | loop fusion | bytes 12582916 | tf_op jit(solution)/shard_map/while/body/eval_jaxpr/jit(dynamic_index_in_dim)/squeeze | solution.py:92
  282.1 0.7 constant_dynamic-slice_fusion.3
  282.8 0.7 fusion.32
  283.5 30.9 %fusion.33 = f32[2,16,1024]{2,1,0:T(8,128)S(1)} fusion(bf16[16,6,2,16,1024]{4,3,2,1,0:T(8,128)(2,1)} %dynamic-slice_bitcast_fusion.2, f32[6]{0:T(128)S(1)} %get-tuple-element.321, bf16[2,16,6,2,16,1024]{5,4,3,2,1,0:T(8,128)(2,1)} %get-tuple-element.316, s32[]{:T(128)S(6)} %select_n.82, f32[]{:T(128)} %bitcast.38, f32[]{:T(128)} %bitcast.39, ...), kind=kLoop, calls=%fused_computation.10.clone.1 | loop fusion | flops 94339072 | bytes 12714048 | tf_op jit(solution)/shard_map/while/body/eval_jaxpr/reduce_sum | solution.py:72
  314.4 0.7 dynamic_slice.75
  315.8 6.8 %dynamic-slice_bitcast_fusion.2 = bf16[16,6,2,16,1024]{4,3,2,1,0:T(8,128)(2,1)} fusion(bf16[2,16,6,2,16,1024]{5,4,3,2,1,0:T(8,128)(2,1)} %get-tuple-element.315, s32[]{:T(128)S(6)} %select_n.80), kind=kLoop, calls=%fused_computation.11.clone.1 | loop fusion | bytes 12582916 | tf_op jit(solution)/shard_map/while/body/eval_jaxpr/jit(dynamic_index_in_dim)/squeeze | solution.py:92
  322.6 0.7 constant_dynamic-slice_fusion.3
  323.2 0.7 fusion.32
  323.9 30.9 %fusion.33 = f32[2,16,1024]{2,1,0:T(8,128)S(1)} fusion(bf16[16,6,2,16,1024]{4,3,2,1,0:T(8,128)(2,1)} %dynamic-slice_bitcast_fusion.2, f32[6]{0:T(128)S(1)} %get-tuple-element.321, bf16[2,16,6,2,16,1024]{5,4,3,2,1,0:T(8,128)(2,1)} %get-tuple-element.316, s32[]{:T(128)S(6)} %select_n.82, f32[]{:T(128)} %bitcast.38, f32[]{:T(128)} %bitcast.39, ...), kind=kLoop, calls=%fused_computation.10.clone.1 | loop fusion | flops 94339072 | bytes 12714048 | tf_op jit(solution)/shard_map/while/body/eval_jaxpr/reduce_sum | solution.py:72
  354.8 0.7 dynamic_slice.75
  356.2 6.8 %dynamic-slice_bitcast_fusion.2 = bf16[16,6,2,16,1024]{4,3,2,1,0:T(8,128)(2,1)} fusion(bf16[2,16,6,2,16,1024]{5,4,3,2,1,0:T(8,128)(2,1)} %get-tuple-element.315, s32[]{:T(128)S(6)} %select_n.80), kind=kLoop, calls=%fused_computation.11.clone.1 | loop fusion | bytes 12582916 | tf_op jit(solution)/shard_map/while/body/eval_jaxpr/jit(dynamic_index_in_dim)/squeeze | solution.py:92
  362.9 0.7 constant_dynamic-slice_fusion.3
  363.6 0.7 fusion.32
  364.3 30.9 %fusion.33 = f32[2,16,1024]{2,1,0:T(8,128)S(1)} fusion(bf16[16,6,2,16,1024]{4,3,2,1,0:T(8,128)(2,1)} %dynamic-slice_bitcast_fusion.2, f32[6]{0:T(128)S(1)} %get-tuple-element.321, bf16[2,16,6,2,16,1024]{5,4,3,2,1,0:T(8,128)(2,1)} %get-tuple-element.316, s32[]{:T(128)S(6)} %select_n.82, f32[]{:T(128)} %bitcast.38, f32[]{:T(128)} %bitcast.39, ...), kind=kLoop, calls=%fused_computation.10.clone.1 | loop fusion | flops 94339072 | bytes 12714048 | tf_op jit(solution)/shard_map/while/body/eval_jaxpr/reduce_sum | solution.py:72
  395.3 0.7 dynamic_slice.75
  396.6 6.8 %dynamic-slice_bitcast_fusion.2 = bf16[16,6,2,16,1024]{4,3,2,1,0:T(8,128)(2,1)} fusion(bf16[2,16,6,2,16,1024]{5,4,3,2,1,0:T(8,128)(2,1)} %get-tuple-element.315, s32[]{:T(128)S(6)} %select_n.80), kind=kLoop, calls=%fused_computation.11.clone.1 | loop fusion | bytes 12582916 | tf_op jit(solution)/shard_map/while/body/eval_jaxpr/jit(dynamic_index_in_dim)/squeeze | solution.py:92
  403.4 0.7 constant_dynamic-slice_fusion.3
  404.1 0.7 fusion.32
  404.8 30.9 %fusion.33 = f32[2,16,1024]{2,1,0:T(8,128)S(1)} fusion(bf16[16,6,2,16,1024]{4,3,2,1,0:T(8,128)(2,1)} %dynamic-slice_bitcast_fusion.2, f32[6]{0:T(128)S(1)} %get-tuple-element.321, bf16[2,16,6,2,16,1024]{5,4,3,2,1,0:T(8,128)(2,1)} %get-tuple-element.316, s32[]{:T(128)S(6)} %select_n.82, f32[]{:T(128)} %bitcast.38, f32[]{:T(128)} %bitcast.39, ...), kind=kLoop, calls=%fused_computation.10.clone.1 | loop fusion | flops 94339072 | bytes 12714048 | tf_op jit(solution)/shard_map/while/body/eval_jaxpr/reduce_sum | solution.py:72
  435.6 0.7 dynamic_slice.75
  437.0 0.7 copy-done.1
  437.7 0.0 all-reduce.6.cloned.1.call-update
  437.7 0.6 dynamic-slice
  438.9 45.3 %all-reduce.6.cloned.1.call-done = f32[2,2,16,1024]{3,2,1,0:T(8,128)} async-done(((f32[2,2,16,1024]{3,2,1,0:T(8,128)}), f32[2,2,16,1024]{3,2,1,0:T(8,128)}) %all-reduce.6.cloned.1.call-update) | async-done | bytes 262160
  484.2 1.5 constant_dynamic-slice_fusion.1
  (17 shorter events, 0.1 us)
Async XLA Ops:
  6.5 477.7 %all-reduce.6.cloned.1.call-start = ((), (), s32[]{:S(2)}) async-start(), calls=%async_computation | async-start | bytes 524288
  6.5 143.1 %collective-permute-start = (bf16[2,16,3,2,16,1024]{5,4,3,2,1,0:T(8,128)(2,1)}, bf16[2,16,3,2,16,1024]{5,4,3,2,1,0:T(8,128)(2,1)}, u32[]{:S(2)}, u32[]{:S(2)}) collective-permute-start(bf16[2,16,3,2,16,1024]{5,4,3,2,1,0:T(8,128)(2,1)} %param.9), channel_id=1, source_target_pairs={{0,1},{1,2},{2,3},{3,4},{4,5},{5,6},{6,7},{7,8},{8,9},{9,10},{10,1... | collective-permute-start | bytes 18874376 | tf_op jit(solution)/shard_map/ppermute | solution.py:14
  9.7 140.8 %collective-permute-start.1 = (bf16[2,16,3,2,16,1024]{5,4,3,2,1,0:T(8,128)(2,1)}, bf16[2,16,3,2,16,1024]{5,4,3,2,1,0:T(8,128)(2,1)}, u32[]{:S(2)}, u32[]{:S(2)}) collective-permute-start(bf16[2,16,3,2,16,1024]{5,4,3,2,1,0:T(8,128)(2,1)} %param.9), channel_id=1, source_target_pairs={{1,0},{2,1},{3,2},{4,3},{5,4},{6,5},{7,6},{8,7},{9,8},{10,9},{11,1... | collective-permute-start | bytes 18874376 | tf_op jit(solution)/shard_map/ppermute | solution.py:15
  202.5 43.5 %copy-start.3 = (f32[2,16,1024]{2,1,0:T(8,128)S(1)}, f32[2,16,1024]{2,1,0:T(8,128)}, u32[]{:S(2)}) copy-start(f32[2,16,1024]{2,1,0:T(8,128)} %param.11) | copy-start | bytes 393220
  252.4 7.0 %copy-start.2 = (f32[2,16,1024]{2,1,0:T(8,128)S(1)}, f32[2,16,1024]{2,1,0:T(8,128)}, u32[]{:S(2)}) copy-start(f32[2,16,1024]{2,1,0:T(8,128)} %param.12) | copy-start | bytes 393220
  252.4 11.7 %slice-start = ((s8[12582912]{0:T(1024)(128)(4,1)}), s8[4194304]{0:T(1024)(128)(4,1)S(1)}, s32[]{:S(2)}) async-start(s8[12582912]{0:T(1024)(128)(4,1)} %bitcast.48), calls=%async_computation.1 | async-start | bytes 8388608
  255.9 8.3 %slice-start.1 = ((s8[12582912]{0:T(1024)(128)(4,1)}), s8[4194304]{0:T(1024)(128)(4,1)S(1)}, s32[]{:S(2)}) async-start(s8[12582912]{0:T(1024)(128)(4,1)} %bitcast.48), calls=%async_computation.2 | async-start | bytes 8388608
  259.4 4.8 slice-start.2
  264.2 11.1 %copy-start.4 = (f32[6]{0:T(128)S(1)}, f32[6]{0:T(128)}, u32[]{:S(2)}) copy-start(f32[6]{0:T(128)} %constant.122.clone..sunk.2) | copy-start | bytes 76
  270.8 4.5 copy-start
  275.3 162.4 %copy-start.5 = (u32[256]{0:T(256)S(1)}, u32[256]{0:T(256)}, u32[]{:S(2)}) copy-start(u32[256]{0:T(256)} %constant.137) | copy-start | bytes 3076
  437.0 0.7 copy-start.1
Sparse Core Ops, SparseCore 0:
  437.8 46.3 all-reduce.5
where the time goes:
time: 496 us; the launch traced here: 493 us
  other arithmetic  245 us (49%)
  waiting for transfers between devices  178 us (36%)
  local copies, waits for them, and re-layouts  43.3 us (9%)
  between operations  14.2 us (3%)
  starting transfers between devices  9.79 us (2%)
    ppermute x1, waiting for transfers between devices, padded_2(): before = lax.ppermute(last, axis, up)  132 us
    reduce_sum x4, other arithmetic, contribution(): jnp.sum(filtered * green_one.astype(jnp.float32) * weights, axis=(0, 1))  124 us
    unnamed x2, waiting for transfers between devices  45.3 us
    div x1, other arithmetic, derivative(): return (8.0 * (window(1) - window(-1)) - (window(2) - window(-2))) / 12.0  43.5 us
    div x1, other arithmetic, depth_derivative(): return (8.0 * (window(1) - window(-1)) - (window(2) - window(-2))) / 12.0  31.8 us
    squeeze x4, local copies, waits for them, and re-layouts, add_slot(): stress_one = lax.dynamic_index_in_dim(stress, source, 0, keepdims=False)  27.1 us
    unnamed x6, other arithmetic  21.3 us
    convert_element_type x1, other arithmetic, on_device(): field = extended.astype(jnp.float32)  20.2 us
  transfers between devices with their start and end apart: 3, of which 3 were waited for; matrix products, arithmetic and copies ran while one was open for 0% of the time, Pallas kernels for 0%

commit v1 on v0

v1 whole, which is shorter than its diff:
```python
import functools

import jax
import jax.numpy as jnp
from jax import lax
from jax.experimental import pallas as pl
from jax.experimental.pallas import tpu as pltpu
from jax.sharding import PartitionSpec as P

MESH = pl.DeviceIdType.MESH
F32, BF16 = jnp.float32, jnp.bfloat16
ROW = 16
LANES = 128
WIDE = 256
RING_X = 4
WINDOW = 2


def iota2(shape, axis):
    return lax.broadcasted_iota(jnp.int32, shape, axis)


def stencil(offset):
    eight = jnp.where(offset == 1, 8.0, jnp.where(offset == -1, -8.0, 0.0))
    return jnp.where(offset == 2, -1.0, jnp.where(offset == -2, 1.0, eight))


def kernel(
    sources, snaps, stations, lags,
    u_hbm, g_hbm, lam_hbm, mu_hbm, filt, pairs, out_ref,
    uv, gv, lamv, muv, halo, dz, adj, hbuf, dxb, dyb, mix_hi, mix_lo, colmat, rowmat, kacc, kpart, red,
    u_sem, g_sem, lam_sem, mu_sem,
    halo_send, halo_recv, sib_send, sib_recv, par_send, par_recv, fwd_send, fwd_recv, red_send, red_recv,
):
    slots = sources * snaps
    quarter = slots // 4
    pieces = dz.shape[0]
    blocks = gv.shape[0]
    cols = u_hbm.shape[-1]

    rcv, slab = lax.axis_index("rcv"), lax.axis_index("slab")
    slabs = lax.axis_size("slab")
    sibling = rcv + 1 - 2 * (rcv % 2)
    partner = (rcv + 2) % 4
    diagonal = (sibling + 2) % 4
    up_rcv = (rcv + 2 * ((slab % RING_X + 1) // RING_X)) % 4
    down_rcv = (rcv + 2 * ((RING_X - slab % RING_X) // RING_X)) % 4
    up = {"slab": (slab + 1) % slabs, "rcv": up_rcv}
    down = {"slab": (slab + slabs - 1) % slabs, "rcv": down_rcv}
    has_below = ((slab + slabs - 1) // slabs).astype(F32)
    has_above = ((2 * slabs - 2 - slab) // slabs).astype(F32)

    u_copy = pltpu.make_async_copy(u_hbm, uv.at[:, :, :, :, pl.ds(LANES, cols)], u_sem)
    u_copy.start()

    def g_copy(block):
        return pltpu.make_async_copy(
            g_hbm.at[:, :, :, :, pl.ds(pl.multiple_of(block * WIDE, WIDE), WIDE)], gv.at[block], g_sem.at[block])

    for block in range(blocks):
        g_copy(block).start()
    lam_copy = pltpu.make_async_copy(lam_hbm, lamv, lam_sem)
    mu_copy = pltpu.make_async_copy(mu_hbm, muv, mu_sem)
    lam_copy.start()
    mu_copy.start()

    barrier = pltpu.get_barrier_semaphore()
    peers = (up, down, {"rcv": sibling}, {"rcv": partner}, {"rcv": diagonal})
    for peer in peers:
        pl.semaphore_signal(barrier, inc=1, device_id=peer, device_id_type=MESH)
    pl.semaphore_wait(barrier, len(peers))

    def halo_copy(side, piece):
        target, their = ((up, up_rcv), (down, down_rcv))[side]
        return pltpu.make_async_remote_copy(
            src_ref=u_hbm.at[pl.ds(their * quarter, quarter), :, :, :, pl.ds(pl.multiple_of(piece * LANES, LANES), LANES)],
            dst_ref=halo.at[side, piece],
            send_sem=halo_send.at[side, piece], recv_sem=halo_recv.at[side, piece],
            device_id=target, device_id_type=MESH)

    def share_copy(piece, of, target, send, recv):
        block = dz.at[piece, pl.ds(of * quarter, quarter)]
        return pltpu.make_async_remote_copy(
            src_ref=block, dst_ref=block, send_sem=send.at[piece], recv_sem=recv.at[piece],
            device_id={"rcv": target}, device_id_type=MESH)

    def to_sibling(piece):
        return share_copy(piece, rcv, sibling, sib_send, sib_recv)

    def to_partner(piece):
        return share_copy(piece, rcv, partner, par_send, par_recv)

    def forward(piece):
        return share_copy(piece, partner, sibling, fwd_send, fwd_recv)

    def red_copy(which, piece):
        target = (sibling, partner, diagonal)[which]
        return pltpu.make_async_remote_copy(
            src_ref=kpart.at[piece, target], dst_ref=red.at[which, piece],
            send_sem=red_send.at[which, piece], recv_sem=red_recv.at[which, piece],
            device_id={"rcv": target}, device_id_type=MESH)

    for piece in range(WINDOW):
        for side in range(2):
            halo_copy(side, piece).start()

    a, b = iota2((slots, stations * snaps), 0), iota2((slots, stations * snaps), 1)
    lag = a % snaps - b % snaps + lags // 2
    taps = jnp.zeros((slots, stations * snaps), F32)
    for source in range(sources):
        for station in range(stations):
            used = pairs[source, station].astype(F32)
            here = (a // snaps == source) & (b // snaps == station)
            for j in range(lags):
                taps = taps + jnp.where(here & (lag == j), filt[source, station, j] * used, 0.0)
    high = taps.astype(BF16)
    low = (taps - high.astype(F32)).astype(BF16)
    size = slots * ROW
    spread = (iota2((size, slots), 0) // ROW == iota2((size, slots), 1)).astype(BF16)
    depth = stations * snaps * ROW
    spread_t = (iota2((stations * snaps, depth), 0) == iota2((stations * snaps, depth), 1) // ROW).astype(BF16)
    same_row = iota2((size, depth), 0) % ROW == iota2((size, depth), 1) % ROW
    for part, target in ((high, mix_hi), (low, mix_lo)):
        tall = jnp.dot(spread, part, preferred_element_type=F32).astype(BF16)
        target[...] = jnp.where(same_row, jnp.dot(tall, spread_t, preferred_element_type=F32), 0.0).astype(BF16)
    i, o = iota2(colmat.shape, 0), iota2(colmat.shape, 1)
    colmat[...] = stencil(i - LANES - o).astype(BF16)
    i, o = iota2(rowmat.shape, 1), iota2(rowmat.shape, 0)
    rowmat[...] = jnp.where(i // ROW == o // ROW, stencil(i - o), 0.0).astype(BF16)
    edge = jnp.zeros(uv.shape[:-1] + (LANES,), BF16)
    u_copy.wait()
    uv[:, :, :, :, :LANES] = edge
    uv[:, :, :, :, LANES + cols:] = edge
    lam_copy.wait()
    mu_copy.wait()

    half = slots // 2

    def early(step):
        block, plane = step // 2, step % 2
        slot = block % 2

        @pl.when(plane == 0)
        def _():
            g_copy(block).wait()

        def mix(c, _):
            g = gv[block, :, c, plane].reshape(depth, WIDE)
            hbuf[c] = (jnp.dot(mix_hi[...], g, preferred_element_type=F32)
                       + jnp.dot(mix_lo[...], g, preferred_element_type=F32))
            return 0

        lax.fori_loop(0, 6, mix, 0)
        start = pl.multiple_of(block * WIDE, WIDE)

        def derive(k, _):
            around = uv[:, k, plane, :, pl.ds(start, 2 * WIDE)].reshape(size, 2 * WIDE)
            dxb[k] = jnp.dot(around, colmat[...], preferred_element_type=F32)
            inside = pl.ds(pl.multiple_of(start + LANES, LANES), WIDE)
            for part in range(2):
                rows = uv[part * half:(part + 1) * half, k, plane, :, inside].reshape(half * ROW, WIDE)
                dyb[k, part * half * ROW:(part + 1) * half * ROW] = jnp.dot(
                    rowmat[...], rows, preferred_element_type=F32)
            return 0

        lax.fori_loop(0, 3, derive, 0)
        lam = lamv[plane, :, pl.ds(start, WIDE)]
        shear = 2.0 * muv[plane, :, pl.ds(start, WIDE)]

        for source in range(sources):
            def weigh(t, carry):
                trace, rest = carry
                at = source * snaps + t
                here = pl.ds(pl.multiple_of(at * ROW, ROW), ROW)
                h = [hbuf[c, here] for c in range(6)]
                dx = [dxb[k, here] for k in range(3)]
                dy = [dyb[k, here] for k in range(3)]
                total = h[0] + h[1] + h[2]
                trace = trace + (dx[0] + dy[1]) * total
                rest = rest + (dx[0] * h[0] + dy[1] * h[1] + dy[2] * h[3] + dx[2] * h[4] + (dy[0] + dx[1]) * h[5])
                for k, value in enumerate((shear * h[4], shear * h[3], lam * total + shear * h[2])):
                    for side in range(2):
                        adj[slot, side, k, at, plane] = value[:, side * LANES:(side + 1) * LANES]
                return trace, rest

            zero = jnp.zeros((ROW, WIDE), F32)
            trace, rest = lax.fori_loop(0, snaps, weigh, (zero, zero))
            value = lam * trace + shear * rest
            for side in range(2):
                kacc[2 * block + side, source, plane] = value[:, side * LANES:(side + 1) * LANES]

    def depth_derivative(piece):
        here = pl.ds(pl.multiple_of(LANES + piece * LANES, LANES), LANES)

        def one(n, _):
            at = rcv * quarter + n
            for k in range(3):
                f0, f1 = (uv[at, k, plane, :, here].astype(F32) for plane in range(2))
                b0, b1 = (has_below * halo[0, piece, n, k, plane].astype(F32) for plane in range(2))
                a0, a1 = (has_above * halo[1, piece, n, k, plane].astype(F32) for plane in range(2))
                dz[piece, at, k, 0] = (8.0 * (f1 - b1) - (a0 - b0)).astype(BF16)
                dz[piece, at, k, 1] = (8.0 * (a0 - f0) - (a1 - b1)).astype(BF16)
            return 0

        lax.fori_loop(0, quarter, one, 0)

    def late(piece):
        slot, side = (piece // 2) % 2, piece % 2
        for source in range(sources):
            def add(t, totals):
                at = source * snaps + t
                new = []
                for plane in range(2):
                    total = totals[plane]
                    for k in range(3):
                        total = total + dz[piece, at, k, plane].astype(F32) * adj[slot, side, k, at, plane]
                    new.append(total)
                return tuple(new)

            totals = lax.fori_loop(0, snaps, add, tuple(kacc[piece, source, plane] for plane in range(2)))
            for plane in range(2):
                value = totals[plane] * (1.0 / 12.0)
                for owner in range(4):
                    kpart[piece, owner, source, plane] = value[owner * (ROW // 4):(owner + 1) * (ROW // 4)]

    def step(s, _):
        @pl.when(s < pieces)
        def _():
            early(s)
            for side in range(2):
                halo_copy(side, s).wait()
            @pl.when(s + WINDOW < pieces)
            def _():
                for side in range(2):
                    halo_copy(side, s + WINDOW).start()
            depth_derivative(s)
            to_partner(s).start()
            to_sibling(s).start()

        @pl.when((s >= 1) & (s <= pieces))
        def _():
            to_partner(s - 1).wait()
            forward(s - 1).start()

        @pl.when(s >= 2)
        def _():
            to_sibling(s - 2).wait()
            forward(s - 2).wait()
            late(s - 2)
            for which in range(3):
                red_copy(which, s - 2).start()
        return 0

    lax.fori_loop(0, pieces + 2, step, 0)

    for piece in range(pieces):
        for which in range(3):
            red_copy(which, piece).wait()
        out_ref[:, :, :, piece * LANES:(piece + 1) * LANES] = (
            (kpart[piece, rcv] + red[0, piece]) + (red[1, piece] + red[2, piece]))


def on_device(displacement, green, lame_lambda, shear_modulus, filters, pairs):
    sources, snaps, parts, planes, rows, cols = displacement.shape
    stations, lags = filters.shape[1:]
    slots, taps = sources * snaps, stations * snaps
    pieces, blocks, quarter = cols // LANES, cols // WIDE, slots // 4
    size, depth = slots * ROW, taps * ROW
    anywhere = pl.BlockSpec(memory_space=pl.ANY)
    scalars = pl.BlockSpec(memory_space=pltpu.SMEM)
    dma = pltpu.SemaphoreType.DMA
    return pl.pallas_call(
        functools.partial(kernel, sources, snaps, stations, lags),
        out_shape=jax.ShapeDtypeStruct((sources, planes, rows // 4, cols), F32),
        in_specs=[anywhere] * 4 + [scalars] * 2,
        out_specs=pl.BlockSpec(memory_space=pltpu.VMEM),
        scratch_shapes=[
            pltpu.VMEM((slots, parts, planes, rows, cols + 2 * LANES), BF16),
            pltpu.VMEM((blocks, taps, 6, planes, rows, WIDE), BF16),
            pltpu.VMEM((planes, rows, cols), F32),
            pltpu.VMEM((planes, rows, cols), F32),
            pltpu.VMEM((2, pieces, quarter, parts, planes, rows, LANES), BF16),
            pltpu.VMEM((pieces, slots, parts, planes, rows, LANES), BF16),
            pltpu.VMEM((2, 2, parts, slots, planes, rows, LANES), F32),
            pltpu.VMEM((6, size, WIDE), F32),
            pltpu.VMEM((3, size, WIDE), F32),
            pltpu.VMEM((3, size, WIDE), F32),
            pltpu.VMEM((size, depth), BF16),
            pltpu.VMEM((size, depth), BF16),
            pltpu.VMEM((2 * WIDE, WIDE), BF16),
            pltpu.VMEM((size // 2, size // 2), BF16),
            pltpu.VMEM((pieces, sources, planes, rows, LANES), F32),
            pltpu.VMEM((pieces, 4, sources, planes, rows // 4, LANES), F32),
            pltpu.VMEM((3, pieces, sources, planes, rows // 4, LANES), F32),
            dma, dma((blocks,)), dma, dma,
            dma((2, pieces)), dma((2, pieces)),
            dma((pieces,)), dma((pieces,)), dma((pieces,)), dma((pieces,)), dma((pieces,)), dma((pieces,)),
            dma((3, pieces)), dma((3, pieces)),
        ],
        compiler_params=pltpu.CompilerParams(
            collective_id=0, has_side_effects=True, vmem_limit_bytes=60 << 20),
        cost_estimate=pl.CostEstimate(flops=26_000_000_000, bytes_accessed=20_000_000, transcendentals=0),
    )(
        displacement.reshape(slots, parts, planes, rows, cols),
        green.reshape(taps, 6, planes, rows, cols),
        lame_lambda, shear_modulus, filters, pairs,
    )


def solution(mesh):
    placed = (
        P(None, None, None, "slab", None, None),
        P("rcv", None, None, "slab", None, None),
        P("slab", None, None),
        P("slab", None, None),
        P(None, "rcv", None),
        P(None, "rcv"),
    )
    return jax.shard_map(
        on_device,
        mesh=mesh,
        in_specs=placed,
        out_specs=P(None, "slab", "rcv", None),
        check_vma=False,
    )
```

time: 496 us -> 68 us (0.14)
  the two profiles are of different devices: /device:TPU:161 before, /device:TPU:1 now
where the time goes in v1:
time: 68 us; the launch traced here: 67.8 us
  Pallas kernels  66.3 us (98%)
  local copies, waits for them, and re-layouts  1.47 us (2%)
    pallas_call x1, Pallas kernels, on_device(): pl.pallas_call(functools.partial(kernel, sources, snaps, stations, lags),...  66.3 us
    unnamed x1, local copies, waits for them, and re-layouts  1.47 us

profile of v1, /device:TPU:1, one launch (start us, length us, event | category | flops | bytes accessed | tf_op | source)
XLA Modules:
  0.0 67.8 jit_solution(17983739544930240933)
XLA Ops:
  0.0 66.3 %shard_map.64 = f32[2,2,4,1024]{3,2,1,0:T(4,128)} custom-call(bf16[32,3,2,16,1024]{4,3,2,1,0:T(8,128)(2,1)} %bitcast.3, bf16[32,6,2,16,1024]{4,3,2,1,0:T(8,128)(2,1)} %bitcast.2, f32[2,16,1024]{2,1,0:T(8,128)} %lam_hbm.1, f32[2,16,1024]{2,1,0:T(8,128)} %mu_hbm.1, f32[2,2,9]{2,1,0:T(2,128)} %filt.1, s32[2,2]{1,0:T(2,128)} %pairs.1), custom_call_target="tpu_custom_call" | custom-call | flops 25999998976 | bytes 20000000 | tf_op jit(solution)/shard_map/pallas_call | solution.py:272
  66.3 1.5 %copy.8 = f32[2,2,4,1024]{3,2,1,0:T(4,128)} copy(f32[2,2,4,1024]{3,2,1,0:T(4,128)} %shard_map.64) | data formatting | bytes 131072

commit v2 on v1

v2 whole, which is shorter than its diff:
```python
import functools

import jax
import jax.numpy as jnp
from jax import lax
from jax.experimental import pallas as pl
from jax.experimental.pallas import tpu as pltpu
from jax.sharding import PartitionSpec as P

MESH = pl.DeviceIdType.MESH
F32, BF16 = jnp.float32, jnp.bfloat16
ROW = 16
LANES = 128
WIDE = 256
RING_X = 4
HALF = ROW // 2
CUTS = 2


def iota2(shape, axis):
    return lax.broadcasted_iota(jnp.int32, shape, axis)


def stencil(offset):
    eight = jnp.where(offset == 1, 8.0, jnp.where(offset == -1, -8.0, 0.0))
    return jnp.where(offset == 2, -1.0, jnp.where(offset == -2, 1.0, eight))


def kernel(
    sources, snaps, stations, lags,
    u_hbm, g_hbm, lam_hbm, mu_hbm, filt, pairs, out_ref,
    uv, gv, lamv, muv, halo, dz, adj, hbuf, dxb, dyb, mixer, colmat, rowmat, kacc, kpart, red,
    u_sem, g_sem, lam_sem, mu_sem,
    halo_send, halo_recv, sib_send, sib_recv, par_send, par_recv, fwd_send, fwd_recv, red_send, red_recv,
):
    slots = sources * snaps
    quarter = slots // 4
    cut = quarter // CUTS
    pieces = dz.shape[0]
    blocks = gv.shape[0]
    cols = u_hbm.shape[-1]

    rcv, slab = lax.axis_index("rcv"), lax.axis_index("slab")
    slabs = lax.axis_size("slab")
    sibling = rcv + 1 - 2 * (rcv % 2)
    partner = (rcv + 2) % 4
    diagonal = (sibling + 2) % 4
    up_rcv = (rcv + 2 * ((slab % RING_X + 1) // RING_X)) % 4
    down_rcv = (rcv + 2 * ((RING_X - slab % RING_X) // RING_X)) % 4
    up = {"slab": (slab + 1) % slabs, "rcv": up_rcv}
    down = {"slab": (slab + slabs - 1) % slabs, "rcv": down_rcv}
    has_above, has_below = slab < slabs - 1, slab > 0
    count_above, count_below = (2 * slabs - 2 - slab) // slabs, (slabs - 1 + slab) // slabs

    u_copy = pltpu.make_async_copy(u_hbm, uv.at[:, :, :, :, pl.ds(LANES, cols)], u_sem)

    def g_copy(block):
        return pltpu.make_async_copy(
            g_hbm.at[:, :, :, :, pl.ds(pl.multiple_of(block * WIDE, WIDE), WIDE)], gv.at[block], g_sem.at[block])

    g_copy(0).start()
    u_copy.start()
    for block in range(1, blocks):
        g_copy(block).start()
    lam_copy = pltpu.make_async_copy(lam_hbm, lamv, lam_sem)
    mu_copy = pltpu.make_async_copy(mu_hbm, muv, mu_sem)
    lam_copy.start()
    mu_copy.start()

    barrier = pltpu.get_barrier_semaphore()
    def greet(peer):
        pl.semaphore_signal(barrier, inc=1, device_id=peer, device_id_type=MESH)

    def at_sides(condition_up, condition_down, act):
        for side, condition in enumerate((condition_up, condition_down)):
            @pl.when(condition)
            def _(side=side):
                act(side)

    at_sides(has_above, has_below, lambda side: greet((up, down)[side]))
    for peer in (sibling, partner, diagonal):
        greet({"rcv": peer})
    pl.semaphore_wait(barrier, 3 + count_above + count_below)

    def halo_copy(side, piece, part):
        target, their = ((up, up_rcv), (down, down_rcv))[side]
        return pltpu.make_async_remote_copy(
            src_ref=u_hbm.at[pl.ds(their * quarter + part * cut, cut), :, :, :,
                             pl.ds(pl.multiple_of(piece * LANES, LANES), LANES)],
            dst_ref=halo.at[side, piece, pl.ds(part * cut, cut)],
            send_sem=halo_send.at[side], recv_sem=halo_recv.at[side, piece, part],
            device_id=target, device_id_type=MESH)

    def share_copy(piece, part, of, target, send, recv):
        block = dz.at[piece, pl.ds(of * quarter + part * cut, cut)]
        return pltpu.make_async_remote_copy(
            src_ref=block, dst_ref=block, send_sem=send, recv_sem=recv.at[piece, part],
            device_id={"rcv": target}, device_id_type=MESH)

    def to_sibling(piece, part):
        return share_copy(piece, part, rcv, sibling, sib_send, sib_recv)

    def to_partner(piece, part):
        return share_copy(piece, part, rcv, partner, par_send, par_recv)

    def forward(piece, part):
        return share_copy(piece, part, partner, sibling, fwd_send, fwd_recv)

    def red_copy(which, piece):
        target = (sibling, partner, diagonal)[which]
        return pltpu.make_async_remote_copy(
            src_ref=kpart.at[piece, target], dst_ref=red.at[which, piece],
            send_sem=red_send, recv_sem=red_recv.at[which],
            device_id={"rcv": target}, device_id_type=MESH)

    def send_halo(side):
        for piece in range(pieces):
            for part in range(CUTS):
                halo_copy(side, piece, part).start()

    at_sides(has_above, has_below, send_halo)

    def blank(side):
        halo[side] = jnp.zeros(halo.shape[1:], BF16)

    at_sides(slab == 0, slab == slabs - 1, blank)

    a, b = iota2((slots, stations * snaps), 0), iota2((slots, stations * snaps), 1)
    lag = (a & (snaps - 1)) - (b & (snaps - 1)) + lags // 2
    taps = jnp.zeros((slots, stations * snaps), F32)
    for source in range(sources):
        for station in range(stations):
            used = pairs[source, station].astype(F32)
            here = ((a // snaps) == source) & ((b // snaps) == station)
            for j in range(lags):
                taps = taps + jnp.where(here & (lag == j), filt[source, station, j] * used, 0.0)
    high = taps.astype(BF16)
    low = (taps - high.astype(F32)).astype(BF16)
    size, depth = slots * HALF, stations * snaps * HALF
    spread = ((iota2((size, slots), 0) >> 3) == iota2((size, slots), 1)).astype(BF16)
    spread_t = (iota2((stations * snaps, depth), 0) == (iota2((stations * snaps, depth), 1) >> 3)).astype(BF16)
    same_row = ((iota2((size, depth), 0) ^ iota2((size, depth), 1)) & (HALF - 1)) == 0
    for n, part in enumerate((high, low)):
        tall = jnp.dot(spread, part, preferred_element_type=F32).astype(BF16)
        mixer[n * size:(n + 1) * size] = jnp.where(
            same_row, jnp.dot(tall, spread_t, preferred_element_type=F32), 0.0).astype(BF16)
    i, o = iota2(colmat.shape, 0), iota2(colmat.shape, 1)
    colmat[...] = stencil(i - LANES - o).astype(BF16)
    i, o = iota2(rowmat.shape, 1), iota2(rowmat.shape, 0)
    rowmat[...] = jnp.where((i >> 4) == (o >> 4), stencil(i - o), 0.0).astype(BF16)
    lam_copy.wait()
    mu_copy.wait()

    half = slots // 2

    def early(step):
        block, plane = step // 2, step % 2
        slot = block % 2

        @pl.when(plane == 0)
        def _():
            g_copy(block).wait()

        for c in range(6):
            g = gv[block, :, c, plane].astype(F32)
            for part in range(2):
                rows = g[:, part * HALF:(part + 1) * HALF].reshape(depth, WIDE).astype(BF16)
                both = jnp.dot(mixer[...], rows, preferred_element_type=F32)
                hbuf[c, part] = both[:size] + both[size:]
        start = pl.multiple_of(block * WIDE, WIDE)

        @pl.when(step == 0)
        def _():
            edge = jnp.zeros(uv.shape[:-1] + (LANES,), BF16)
            u_copy.wait()
            uv[:, :, :, :, :LANES] = edge
            uv[:, :, :, :, LANES + cols:] = edge

        for k in range(3):
            around = uv[:, k, plane, :, pl.ds(start, 2 * WIDE)].reshape(slots * ROW, 2 * WIDE)
            dxb[k] = jnp.dot(around, colmat[...], preferred_element_type=F32)
            inside = pl.ds(pl.multiple_of(start + LANES, LANES), WIDE)
            for part in range(2):
                rows = uv[part * half:(part + 1) * half, k, plane, :, inside].reshape(half * ROW, WIDE)
                dyb[k, part * half * ROW:(part + 1) * half * ROW] = jnp.dot(
                    rowmat[...], rows, preferred_element_type=F32)
        lam = lamv[plane, :, pl.ds(start, WIDE)]
        shear = 2.0 * muv[plane, :, pl.ds(start, WIDE)]

        for source in range(sources):
            def weigh(t, carry):
                trace, rest = carry
                at = source * snaps + t
                here = pl.ds(pl.multiple_of(at * ROW, ROW), ROW)
                rows = pl.ds(pl.multiple_of(at * HALF, HALF), HALF)
                h = [jnp.concatenate([hbuf[c, 0, rows], hbuf[c, 1, rows]], axis=0) for c in range(6)]
                dx = [dxb[k, here] for k in range(3)]
                dy = [dyb[k, here] for k in range(3)]
                total = h[0] + h[1] + h[2]
                trace = trace + (dx[0] + dy[1]) * total
                rest = rest + (dx[0] * h[0] + dy[1] * h[1] + dy[2] * h[3] + dx[2] * h[4] + (dy[0] + dx[1]) * h[5])
                for k, value in enumerate((shear * h[4], shear * h[3], lam * total + shear * h[2])):
                    for side in range(2):
                        adj[slot, side, k, at, plane] = value[:, side * LANES:(side + 1) * LANES]
                return trace, rest

            zero = jnp.zeros((ROW, WIDE), F32)
            trace, rest = lax.fori_loop(0, snaps, weigh, (zero, zero), unroll=2)
            value = lam * trace + shear * rest
            for side in range(2):
                kacc[2 * block + side, source, plane] = value[:, side * LANES:(side + 1) * LANES]

    def depth_derivative(piece, part):
        here = pl.ds(pl.multiple_of(LANES + piece * LANES, LANES), LANES)

        def one(n, _):
            n = part * cut + n
            at = rcv * quarter + n
            for k in range(3):
                f0, f1 = (uv[at, k, plane, :, here].astype(F32) for plane in range(2))
                b0, b1 = (halo[0, piece, n, k, plane].astype(F32) for plane in range(2))
                a0, a1 = (halo[1, piece, n, k, plane].astype(F32) for plane in range(2))
                dz[piece, at, k, 0] = (8.0 * (f1 - b1) - (a0 - b0)).astype(BF16)
                dz[piece, at, k, 1] = (8.0 * (a0 - f0) - (a1 - b1)).astype(BF16)
            return 0

        lax.fori_loop(0, cut, one, 0, unroll=True)

    def late(piece, of):
        slot, side = (piece // 2) % 2, piece % 2
        source = of * quarter // snaps

        def add(n, totals):
            at = of * quarter + n
            new = []
            for plane in range(2):
                terms = [dz[piece, at, k, plane].astype(F32) * adj[slot, side, k, at, plane] for k in range(3)]
                new.append(totals[plane] + (terms[0] + terms[1] + terms[2]))
            return tuple(new)

        totals = lax.fori_loop(0, quarter, add, tuple(kacc[piece, source, plane] for plane in range(2)), unroll=True)
        for plane in range(2):
            kacc[piece, source, plane] = totals[plane]

    def hand_out(piece):
        for source in range(sources):
            for plane in range(2):
                value = kacc[piece, source, plane] * (1.0 / 12.0)
                for owner in range(4):
                    kpart[piece, owner, source, plane] = value[owner * (ROW // 4):(owner + 1) * (ROW // 4)]
        for which in range(3):
            red_copy(which, piece).start()

    def step(s, _):
        @pl.when(s < pieces)
        def _():
            early(s)
            for part in range(CUTS):
                at_sides(has_below, has_above, lambda side: halo_copy(side, s, part).wait_recv())
                depth_derivative(s, part)
                to_partner(s, part).start()
                to_sibling(s, part).start()

        @pl.when(s >= 2)
        def _():
            for part in range(CUTS):
                to_sibling(s - 2, part).wait_recv()
            for of in (rcv, sibling, partner):
                late(s - 2, of)
            for part in range(CUTS):
                forward(s - 2, part).wait_recv()
            late(s - 2, diagonal)
            hand_out(s - 2)

        @pl.when((s >= 1) & (s <= pieces))
        def _():
            for part in range(CUTS):
                to_partner(s - 1, part).wait_recv()
                forward(s - 1, part).start()
        return 0

    lax.fori_loop(0, pieces + 2, step, 0)

    def all_sent(block, sem):
        pltpu.make_async_remote_copy(
            src_ref=block, dst_ref=block, send_sem=sem, recv_sem=sem,
            device_id={"rcv": sibling}, device_id_type=MESH).wait_send()

    at_sides(has_above, has_below, lambda side: all_sent(halo.at[side], halo_send.at[side]))
    for sem in (sib_send, par_send, fwd_send):
        all_sent(dz.at[:, pl.ds(rcv * quarter, quarter)], sem)
    all_sent(red, red_send)
    for which in range(3):
        pltpu.make_async_copy(red.at[which], red.at[which], red_recv.at[which]).wait()
    for piece in range(pieces):
        out_ref[:, :, :, piece * LANES:(piece + 1) * LANES] = (
            (kpart[piece, rcv] + red[0, piece]) + (red[1, piece] + red[2, piece]))


def on_device(displacement, green, lame_lambda, shear_modulus, filters, pairs):
    sources, snaps, parts, planes, rows, cols = displacement.shape
    stations, lags = filters.shape[1:]
    slots, taps = sources * snaps, stations * snaps
    pieces, blocks, quarter = cols // LANES, cols // WIDE, slots // 4
    size, depth = slots * ROW, taps * ROW
    anywhere = pl.BlockSpec(memory_space=pl.ANY)
    scalars = pl.BlockSpec(memory_space=pltpu.SMEM)
    dma = pltpu.SemaphoreType.DMA
    return pl.pallas_call(
        functools.partial(kernel, sources, snaps, stations, lags),
        out_shape=jax.ShapeDtypeStruct((sources, planes, rows // 4, cols), F32),
        in_specs=[anywhere] * 4 + [scalars] * 2,
        out_specs=pl.BlockSpec(memory_space=pltpu.VMEM),
        scratch_shapes=[
            pltpu.VMEM((slots, parts, planes, rows, cols + 2 * LANES), BF16),
            pltpu.VMEM((blocks, taps, 6, planes, rows, WIDE), BF16),
            pltpu.VMEM((planes, rows, cols), F32),
            pltpu.VMEM((planes, rows, cols), F32),
            pltpu.VMEM((2, pieces, quarter, parts, planes, rows, LANES), BF16),
            pltpu.VMEM((pieces, slots, parts, planes, rows, LANES), BF16),
            pltpu.VMEM((2, 2, parts, slots, planes, rows, LANES), F32),
            pltpu.VMEM((6, 2, size // 2, WIDE), F32),
            pltpu.VMEM((3, size, WIDE), F32),
            pltpu.VMEM((3, size, WIDE), F32),
            pltpu.VMEM((size, depth // 2), BF16),
            pltpu.VMEM((2 * WIDE, WIDE), BF16),
            pltpu.VMEM((size // 2, size // 2), BF16),
            pltpu.VMEM((pieces, sources, planes, rows, LANES), F32),
            pltpu.VMEM((pieces, 4, sources, planes, rows // 4, LANES), F32),
            pltpu.VMEM((3, pieces, sources, planes, rows // 4, LANES), F32),
            dma, dma((blocks,)), dma, dma,
            dma((2,)), dma((2, pieces, CUTS)),
            dma, dma((pieces, CUTS)), dma, dma((pieces, CUTS)), dma, dma((pieces, CUTS)),
            dma, dma((3,)),
        ],
        compiler_params=pltpu.CompilerParams(
            collective_id=0, has_side_effects=True, vmem_limit_bytes=60 << 20),
        cost_estimate=pl.CostEstimate(flops=26_000_000_000, bytes_accessed=20_000_000, transcendentals=0),
    )(
        displacement.reshape(slots, parts, planes, rows, cols),
        green.reshape(taps, 6, planes, rows, cols),
        lame_lambda, shear_modulus, filters, pairs,
    )


def solution(mesh):
    placed = (
        P(None, None, None, "slab", None, None),
        P("rcv", None, None, "slab", None, None),
        P("slab", None, None),
        P("slab", None, None),
        P(None, "rcv", None),
        P(None, "rcv"),
    )
    return jax.shard_map(
        on_device,
        mesh=mesh,
        in_specs=placed,
        out_specs=P(None, "slab", "rcv", None),
        check_vma=False,
    )
```

time: 68 us -> 55.7 us (0.82)
  the two profiles are of different devices: /device:TPU:1 before, /device:TPU:161 now
where the time goes in v2:
time: 55.7 us; the launch traced here: 55.1 us
  Pallas kernels  53.7 us (96%)
  local copies, waits for them, and re-layouts  1.47 us (3%)
    pallas_call x1, Pallas kernels, on_device(): pl.pallas_call(functools.partial(kernel, sources, snaps, stations, lags),...  53.7 us
    unnamed x1, local copies, waits for them, and re-layouts  1.47 us

profile of v2, /device:TPU:161, one launch (start us, length us, event | category | flops | bytes accessed | tf_op | source)
XLA Modules:
  0.0 55.1 jit_solution(9694255602411028374)
XLA Ops:
  0.0 53.7 %shard_map.64 = f32[2,2,4,1024]{3,2,1,0:T(4,128)} custom-call(bf16[32,3,2,16,1024]{4,3,2,1,0:T(8,128)(2,1)} %bitcast.3, bf16[32,6,2,16,1024]{4,3,2,1,0:T(8,128)(2,1)} %bitcast.2, f32[2,16,1024]{2,1,0:T(8,128)} %lam_hbm.1, f32[2,16,1024]{2,1,0:T(8,128)} %mu_hbm.1, f32[2,2,9]{2,1,0:T(2,128)} %filt.1, s32[2,2]{1,0:T(2,128)} %pairs.1), custom_call_target="tpu_custom_call" | custom-call | flops 25999998976 | bytes 20000000 | tf_op jit(solution)/shard_map/pallas_call | solution.py:309
  53.7 1.5 %copy.8 = f32[2,2,4,1024]{3,2,1,0:T(4,128)} copy(f32[2,2,4,1024]{3,2,1,0:T(4,128)} %shard_map.64) | data formatting | bytes 131072

commit v3 on v2

v3 whole, which is shorter than its diff:
```python
import functools

import jax
import jax.numpy as jnp
from jax import lax
from jax.experimental import pallas as pl
from jax.experimental.pallas import tpu as pltpu
from jax.sharding import PartitionSpec as P

MESH = pl.DeviceIdType.MESH
F32, BF16 = jnp.float32, jnp.bfloat16
ROW = 16
LANES = 128
WIDE = 256
RING_X = 4
HALF = ROW // 2
FIRST = 3


def iota2(shape, axis):
    return lax.broadcasted_iota(jnp.int32, shape, axis)


def stencil(offset):
    eight = jnp.where(offset == 1, 8.0, jnp.where(offset == -1, -8.0, 0.0))
    return jnp.where(offset == 2, -1.0, jnp.where(offset == -2, 1.0, eight))


def kernel(
    sources, snaps, stations, lags,
    u_hbm, g_hbm, lam_hbm, mu_hbm, filt, pairs, out_ref,
    uv, gv, lamv, muv, halo, adj, from_sib, to_par, from_par, hbuf, dxb, dyb, mixer, colmat, rowmat, kacc, kpart, red,
    u_sem, g_sem, lam_sem, mu_sem,
    halo_send, halo_recv, sib_send, sib_recv, par_send, par_recv, red_send, red_recv,
):
    slots = sources * snaps
    quarter = slots // 4
    pieces = halo.shape[1]
    blocks = gv.shape[0]
    steps = adj.shape[0]
    cols = u_hbm.shape[-1]

    rcv, slab = lax.axis_index("rcv"), lax.axis_index("slab")
    slabs = lax.axis_size("slab")
    sibling = rcv + 1 - 2 * (rcv % 2)
    partner = (rcv + 2) % 4
    diagonal = (sibling + 2) % 4
    core, chip = rcv % 2, rcv // 2

    def first_of(device):
        return device % 2 * snaps + device // 2 * quarter

    up_rcv = (rcv + 2 * ((slab % RING_X + 1) // RING_X)) % 4
    down_rcv = (rcv + 2 * ((RING_X - slab % RING_X) // RING_X)) % 4
    up = {"slab": (slab + 1) % slabs, "rcv": up_rcv}
    down = {"slab": (slab + slabs - 1) % slabs, "rcv": down_rcv}
    has_above, has_below = slab < slabs - 1, slab > 0
    count_above, count_below = (2 * slabs - 2 - slab) // slabs, (slabs - 1 + slab) // slabs

    u_copy = pltpu.make_async_copy(u_hbm, uv.at[:, :, :, :, pl.ds(LANES, cols)], u_sem)

    def g_copy(step):
        block, plane = step // 2, step % 2
        return pltpu.make_async_copy(
            g_hbm.at[:, :, plane, :, pl.ds(pl.multiple_of(block * WIDE, WIDE), WIDE)], gv.at[block, :, :, plane],
            g_sem.at[step])

    g_copy(0).start()
    lam_copy = pltpu.make_async_copy(lam_hbm, lamv, lam_sem)
    mu_copy = pltpu.make_async_copy(mu_hbm, muv, mu_sem)
    lam_copy.start()
    mu_copy.start()

    barrier = pltpu.get_barrier_semaphore()
    def greet(peer):
        pl.semaphore_signal(barrier, inc=1, device_id=peer, device_id_type=MESH)

    def at_sides(condition_up, condition_down, act):
        for side, condition in enumerate((condition_up, condition_down)):
            @pl.when(condition)
            def _(side=side):
                act(side)

    at_sides(has_above, has_below, lambda side: greet((up, down)[side]))
    for peer in (sibling, partner, diagonal):
        greet({"rcv": peer})
    def halo_copy(side, piece):
        target, their = ((up, up_rcv), (down, down_rcv))[side]
        return pltpu.make_async_remote_copy(
            src_ref=u_hbm.at[pl.ds(first_of(their), quarter), :, :, :, pl.ds(pl.multiple_of(piece * LANES, LANES), LANES)],
            dst_ref=halo.at[side, piece], send_sem=halo_send.at[side], recv_sem=halo_recv.at[side, piece],
            device_id=target, device_id_type=MESH)

    def to_sibling(step, whose):
        half_of = pl.ds((chip + whose - 2 * chip * whose) * quarter, quarter)
        return pltpu.make_async_remote_copy(
            src_ref=adj.at[step, 1 - core, :, half_of], dst_ref=from_sib.at[step, :, half_of],
            send_sem=sib_send, recv_sem=sib_recv.at[step, whose],
            device_id={"rcv": sibling}, device_id_type=MESH)

    def to_partner(step):
        return pltpu.make_async_remote_copy(
            src_ref=to_par.at[step], dst_ref=from_par.at[step], send_sem=par_send, recv_sem=par_recv.at[step],
            device_id={"rcv": partner}, device_id_type=MESH)

    def red_copy(which, piece):
        target = (sibling, partner, diagonal)[which]
        return pltpu.make_async_remote_copy(
            src_ref=kpart.at[piece, target], dst_ref=red.at[which, piece],
            send_sem=red_send, recv_sem=red_recv.at[which],
            device_id={"rcv": target}, device_id_type=MESH)

    a, b = iota2((slots, stations * snaps), 0), iota2((slots, stations * snaps), 1)
    lag = (a & (snaps - 1)) - (b & (snaps - 1)) + lags // 2
    taps = jnp.zeros((slots, stations * snaps), F32)
    for source in range(sources):
        for station in range(stations):
            used = pairs[source, station].astype(F32)
            here = ((a // snaps) == source) & ((b // snaps) == station)
            for j in range(lags):
                taps = taps + jnp.where(here & (lag == j), filt[source, station, j] * used, 0.0)
    high = taps.astype(BF16)
    low = (taps - high.astype(F32)).astype(BF16)
    size, depth = slots * HALF, stations * snaps * HALF
    spread = ((iota2((size, slots), 0) >> 3) == iota2((size, slots), 1)).astype(BF16)
    spread_t = (iota2((stations * snaps, depth), 0) == (iota2((stations * snaps, depth), 1) >> 3)).astype(BF16)
    same_row = ((iota2((size, depth), 0) ^ iota2((size, depth), 1)) & (HALF - 1)) == 0
    for n, part in enumerate((high, low)):
        tall = jnp.dot(spread, part, preferred_element_type=F32).astype(BF16)
        mixer[n * size:(n + 1) * size] = jnp.where(
            same_row, jnp.dot(tall, spread_t, preferred_element_type=F32), 0.0).astype(BF16)

    pl.semaphore_wait(barrier, 3 + count_above + count_below)

    def send_halo(first, last):
        def send(side):
            for piece in range(first, last):
                halo_copy(side, piece).start()

        at_sides(has_above, has_below, send)

    def blank(side):
        halo[side] = jnp.zeros(halo.shape[1:], BF16)

    send_halo(0, FIRST)
    lam_copy.wait()
    mu_copy.wait()

    half = slots // 2

    def early(step):
        block, plane = step // 2, step % 2

        g_copy(step).wait()

        @pl.when(step == 0)
        def _():
            u_copy.start()

        @pl.when(step + 1 < steps)
        def _():
            g_copy(step + 1).start()

        for c in range(6):
            g = gv[block, :, c, plane].astype(F32)
            for part in range(2):
                rows = g[:, part * HALF:(part + 1) * HALF].reshape(depth, WIDE).astype(BF16)
                both = jnp.dot(mixer[...], rows, preferred_element_type=F32)
                hbuf[c, part] = both[:size] + both[size:]
        start = pl.multiple_of(block * WIDE, WIDE)
        lam = lamv[plane, :, pl.ds(start, WIDE)]
        shear = 2.0 * muv[plane, :, pl.ds(start, WIDE)]

        def mixed(c, at):
            rows = pl.ds(pl.multiple_of(at * HALF, HALF), HALF)
            return jnp.concatenate([hbuf[c, 0, rows], hbuf[c, 1, rows]], axis=0)

        for source in range(sources):
            def turn(t, _):
                h = [mixed(c, source * snaps + t) for c in range(5)]
                adj[step, source, 0, t] = shear * h[4]
                adj[step, source, 1, t] = shear * h[3]
                adj[step, source, 2, t] = lam * (h[0] + h[1] + h[2]) + shear * h[2]
                return 0

            lax.fori_loop(0, snaps, turn, 0, unroll=2)
        to_sibling(step, 1).start()
        to_sibling(step, 0).start()

        @pl.when(step == 0)
        def _():
            send_halo(FIRST, pieces)
            at_sides(slab == 0, slab == slabs - 1, blank)
            i, o = iota2(colmat.shape, 0), iota2(colmat.shape, 1)
            colmat[...] = stencil(i - LANES - o).astype(BF16)
            i, o = iota2(rowmat.shape, 1), iota2(rowmat.shape, 0)
            rowmat[...] = jnp.where((i >> 4) == (o >> 4), stencil(i - o), 0.0).astype(BF16)
            edge = jnp.zeros(uv.shape[:-1] + (LANES,), BF16)
            u_copy.wait()
            uv[:, :, :, :, :LANES] = edge
            uv[:, :, :, :, LANES + cols:] = edge

        for k in range(3):
            around = uv[:, k, plane, :, pl.ds(start, 2 * WIDE)].reshape(slots * ROW, 2 * WIDE)
            dxb[k] = jnp.dot(around, colmat[...], preferred_element_type=F32)
            inside = pl.ds(pl.multiple_of(start + LANES, LANES), WIDE)
            for part in range(2):
                rows = uv[part * half:(part + 1) * half, k, plane, :, inside].reshape(half * ROW, WIDE)
                dyb[k, part * half * ROW:(part + 1) * half * ROW] = jnp.dot(
                    rowmat[...], rows, preferred_element_type=F32)

        to_sibling(step, 1).wait_recv()

        def pass_on(n, _):
            t = (1 - chip) * quarter + n
            for k in range(3):
                to_par[step, k, n] = (adj[step, core, k, t] + from_sib[step, k, t]).astype(BF16)
            return 0

        lax.fori_loop(0, quarter, pass_on, 0, unroll=2)
        to_partner(step).start()

        for source in range(sources):
            def weigh(t, carry):
                trace, rest = carry
                at = source * snaps + t
                here = pl.ds(pl.multiple_of(at * ROW, ROW), ROW)
                h = [mixed(c, at) for c in range(6)]
                dx = [dxb[k, here] for k in range(3)]
                dy = [dyb[k, here] for k in range(3)]
                trace = trace + (dx[0] + dy[1]) * (h[0] + h[1] + h[2])
                rest = rest + (dx[0] * h[0] + dy[1] * h[1] + dy[2] * h[3] + dx[2] * h[4] + (dy[0] + dx[1]) * h[5])
                return trace, rest

            zero = jnp.zeros((ROW, WIDE), F32)
            trace, rest = lax.fori_loop(0, snaps, weigh, (zero, zero), unroll=2)
            value = lam * trace + shear * rest
            for side in range(2):
                kacc[2 * block + side, source, plane] = value[:, side * LANES:(side + 1) * LANES]

    def late(piece):
        block, side = piece // 2, piece % 2
        lanes = pl.ds(pl.multiple_of(side * LANES, LANES), LANES)
        here = pl.ds(pl.multiple_of(LANES + piece * LANES, LANES), LANES)

        def add(n, totals):
            at, t = first_of(rcv) + n, chip * quarter + n
            new = list(totals)
            for k in range(3):
                f0, f1 = (uv[at, k, plane, :, here].astype(F32) for plane in range(2))
                b0, b1 = (halo[0, piece, n, k, plane].astype(F32) for plane in range(2))
                a0, a1 = (halo[1, piece, n, k, plane].astype(F32) for plane in range(2))
                slopes = 8.0 * (f1 - b1) - (a0 - b0), 8.0 * (a0 - f0) - (a1 - b1)
                for plane in range(2):
                    step = 2 * block + plane
                    whole = (adj[step, core, k, t, :, lanes] + from_sib[step, k, t, :, lanes]
                             + from_par[step, k, n, :, lanes].astype(F32))
                    new[plane] = new[plane] + slopes[plane] * whole
            return tuple(new)

        totals = lax.fori_loop(0, quarter, add, tuple(kacc[piece, core, plane] for plane in range(2)), unroll=2)
        for plane in range(2):
            kacc[piece, core, plane] = totals[plane]

    def hand_out(piece):
        for source in range(sources):
            for plane in range(2):
                value = kacc[piece, source, plane] * (1.0 / 12.0)
                for owner in range(4):
                    kpart[piece, owner, source, plane] = value[owner * (ROW // 4):(owner + 1) * (ROW // 4)]
        for which in range(3):
            red_copy(which, piece).start()

    def compute(step, _):
        early(step)
        return 0

    def finish(piece, _):
        @pl.when(piece % 2 == 0)
        def _():
            for plane in range(2):
                to_sibling(2 * (piece // 2) + plane, 0).wait_recv()
                to_partner(2 * (piece // 2) + plane).wait_recv()

        at_sides(has_below, has_above, lambda side: halo_copy(side, piece).wait_recv())
        late(piece)
        hand_out(piece)
        return 0

    lax.fori_loop(0, steps, compute, 0)
    lax.fori_loop(0, pieces, finish, 0)

    def all_sent(block, sem):
        pltpu.make_async_remote_copy(
            src_ref=block, dst_ref=block, send_sem=sem, recv_sem=sem,
            device_id={"rcv": sibling}, device_id_type=MESH).wait_send()

    at_sides(has_above, has_below, lambda side: all_sent(halo.at[side], halo_send.at[side]))
    all_sent(from_sib, sib_send)
    all_sent(from_par, par_send)
    all_sent(red, red_send)
    for which in range(3):
        pltpu.make_async_copy(red.at[which], red.at[which], red_recv.at[which]).wait()
    for piece in range(pieces):
        out_ref[:, :, :, piece * LANES:(piece + 1) * LANES] = (
            (kpart[piece, rcv] + red[0, piece]) + (red[1, piece] + red[2, piece]))


def on_device(displacement, green, lame_lambda, shear_modulus, filters, pairs):
    sources, snaps, parts, planes, rows, cols = displacement.shape
    stations, lags = filters.shape[1:]
    slots, taps = sources * snaps, stations * snaps
    pieces, blocks, quarter = cols // LANES, cols // WIDE, slots // 4
    size, depth, steps = slots * ROW, taps * ROW, blocks * planes
    anywhere = pl.BlockSpec(memory_space=pl.ANY)
    scalars = pl.BlockSpec(memory_space=pltpu.SMEM)
    dma = pltpu.SemaphoreType.DMA
    return pl.pallas_call(
        functools.partial(kernel, sources, snaps, stations, lags),
        out_shape=jax.ShapeDtypeStruct((sources, planes, rows // 4, cols), F32),
        in_specs=[anywhere] * 4 + [scalars] * 2,
        out_specs=pl.BlockSpec(memory_space=pltpu.VMEM),
        scratch_shapes=[
            pltpu.VMEM((slots, parts, planes, rows, cols + 2 * LANES), BF16),
            pltpu.VMEM((blocks, taps, 6, planes, rows, WIDE), BF16),
            pltpu.VMEM((planes, rows, cols), F32),
            pltpu.VMEM((planes, rows, cols), F32),
            pltpu.VMEM((2, pieces, quarter, parts, planes, rows, LANES), BF16),
            pltpu.VMEM((steps, sources, 3, snaps, rows, WIDE), F32),
            pltpu.VMEM((steps, 3, snaps, rows, WIDE), F32),
            pltpu.VMEM((steps, 3, quarter, rows, WIDE), BF16),
            pltpu.VMEM((steps, 3, quarter, rows, WIDE), BF16),
            pltpu.VMEM((6, 2, size // 2, WIDE), F32),
            pltpu.VMEM((3, size, WIDE), F32),
            pltpu.VMEM((3, size, WIDE), F32),
            pltpu.VMEM((size, depth // 2), BF16),
            pltpu.VMEM((2 * WIDE, WIDE), BF16),
            pltpu.VMEM((size // 2, size // 2), BF16),
            pltpu.VMEM((pieces, sources, planes, rows, LANES), F32),
            pltpu.VMEM((pieces, 4, sources, planes, rows // 4, LANES), F32),
            pltpu.VMEM((3, pieces, sources, planes, rows // 4, LANES), F32),
            dma, dma((steps,)), dma, dma,
            dma((2,)), dma((2, pieces)), dma, dma((steps, 2)), dma, dma((steps,)), dma, dma((3,)),
        ],
        compiler_params=pltpu.CompilerParams(
            collective_id=0, has_side_effects=True, vmem_limit_bytes=60 << 20),
        cost_estimate=pl.CostEstimate(flops=26_000_000_000, bytes_accessed=20_000_000, transcendentals=0),
    )(
        displacement.reshape(slots, parts, planes, rows, cols),
        green.reshape(taps, 6, planes, rows, cols),
        lame_lambda, shear_modulus, filters, pairs,
    )


def solution(mesh):
    placed = (
        P(None, None, None, "slab", None, None),
        P("rcv", None, None, "slab", None, None),
        P("slab", None, None),
        P("slab", None, None),
        P(None, "rcv", None),
        P(None, "rcv"),
    )
    return jax.shard_map(
        on_device,
        mesh=mesh,
        in_specs=placed,
        out_specs=P(None, "slab", "rcv", None),
        check_vma=False,
    )
```

time: 55.7 us -> 51.8 us (0.930)
  Pallas kernels: 53.7 us -> 50.1 us
    pallas_call x1, Pallas kernels: 53.7 us -> 50.1 us  [on_device(): pl.pallas_call(functools.partial(kernel, sources, snaps, stations, lags),...]
where the time goes in v3:
time: 51.8 us; the launch traced here: 51.6 us
  Pallas kernels  50.1 us (97%)
  local copies, waits for them, and re-layouts  1.47 us (3%)
    pallas_call x1, Pallas kernels, on_device(): pl.pallas_call(functools.partial(kernel, sources, snaps, stations, lags),...  50.1 us
    unnamed x1, local copies, waits for them, and re-layouts  1.47 us

profile of v3, /device:TPU:161, one launch (start us, length us, event | category | flops | bytes accessed | tf_op | source)
XLA Modules:
  0.0 51.6 jit_solution(14353660999413376912)
XLA Ops:
  0.0 50.1 %shard_map.64 = f32[2,2,4,1024]{3,2,1,0:T(4,128)} custom-call(bf16[32,3,2,16,1024]{4,3,2,1,0:T(8,128)(2,1)} %bitcast.3, bf16[32,6,2,16,1024]{4,3,2,1,0:T(8,128)(2,1)} %bitcast.2, f32[2,16,1024]{2,1,0:T(8,128)} %lam_hbm.1, f32[2,16,1024]{2,1,0:T(8,128)} %mu_hbm.1, f32[2,2,9]{2,1,0:T(2,128)} %filt.1, s32[2,2]{1,0:T(2,128)} %pairs.1), custom_call_target="tpu_custom_call" | custom-call | flops 25999998976 | bytes 20000000 | tf_op jit(solution)/shard_map/pallas_call | solution.py:318
  50.1 1.5 %copy.8 = f32[2,2,4,1024]{3,2,1,0:T(4,128)} copy(f32[2,2,4,1024]{3,2,1,0:T(4,128)} %shard_map.64) | data formatting | bytes 131072

commit v4 on v3

--- a/solution.py
+++ b/solution.py
@@ -15,6 +15,7 @@
 RING_X = 4
 HALF = ROW // 2
 FIRST = 3
+EXTRA = 1
 
 
 def iota2(shape, axis):
@@ -29,9 +30,9 @@
 def kernel(
     sources, snaps, stations, lags,
     u_hbm, g_hbm, lam_hbm, mu_hbm, filt, pairs, out_ref,
-    uv, gv, lamv, muv, halo, adj, from_sib, to_par, from_par, hbuf, dxb, dyb, mixer, colmat, rowmat, kacc, kpart, red,
+    uv, gv, lamv, muv, halo, extra, adj, from_sib, to_par, from_par, hbuf, dxb, dyb, mixer, colmat, rowmat, kacc, kpart, red,
     u_sem, g_sem, lam_sem, mu_sem,
-    halo_send, halo_recv, sib_send, sib_recv, par_send, par_recv, red_send, red_recv,
+    halo_send, halo_recv, extra_send, extra_recv, sib_send, sib_recv, par_send, par_recv, red_send, red_recv,
 ):
     slots = sources * snaps
     quarter = slots // 4
@@ -49,6 +50,9 @@
 
     def first_of(device):
         return device % 2 * snaps + device // 2 * quarter
+
+    def others_of(device):
+        return device % 2 * snaps + (1 - device // 2) * quarter
 
     up_rcv = (rcv + 2 * ((slab % RING_X + 1) // RING_X)) % 4
     down_rcv = (rcv + 2 * ((RING_X - slab % RING_X) // RING_X)) % 4
@@ -91,6 +95,13 @@
             dst_ref=halo.at[side, piece], send_sem=halo_send.at[side], recv_sem=halo_recv.at[side, piece],
             device_id=target, device_id_type=MESH)
 
+    def extra_copy(side, n):
+        target, their = ((up, up_rcv), (down, down_rcv))[side]
+        return pltpu.make_async_remote_copy(
+            src_ref=u_hbm.at[pl.ds(others_of(their), EXTRA), :, :, :, pl.ds((pieces - 2 + n) * LANES, LANES)],
+            dst_ref=extra.at[side, n], send_sem=extra_send.at[side], recv_sem=extra_recv.at[side, n],
+            device_id=target, device_id_type=MESH)
+
     def to_sibling(step, whose):
         half_of = pl.ds((chip + whose - 2 * chip * whose) * quarter, quarter)
         return pltpu.make_async_remote_copy(
@@ -98,9 +109,11 @@
             send_sem=sib_send, recv_sem=sib_recv.at[step, whose],
             device_id={"rcv": sibling}, device_id_type=MESH)
 
-    def to_partner(step):
+    def to_partner(step, skip):
+        part = pl.ds(skip, quarter - skip)
         return pltpu.make_async_remote_copy(
-            src_ref=to_par.at[step], dst_ref=from_par.at[step], send_sem=par_send, recv_sem=par_recv.at[step],
+            src_ref=to_par.at[step, :, part], dst_ref=from_par.at[step, :, part],
+            send_sem=par_send.at[min(skip, 1)], recv_sem=par_recv.at[step],
             device_id={"rcv": partner}, device_id_type=MESH)
 
     def red_copy(which, piece):
@@ -136,13 +149,17 @@
         def send(side):
             for piece in range(first, last):
                 halo_copy(side, piece).start()
+            if last == pieces:
+                for n in range(2):
+                    extra_copy(side, n).start()
 
         at_sides(has_above, has_below, send)
 
     def blank(side):
         halo[side] = jnp.zeros(halo.shape[1:], BF16)
-
-    send_halo(0, FIRST)
+        extra[side] = jnp.zeros(extra.shape[1:], BF16)
+
+    send_halo(0, min(FIRST, pieces))
     lam_copy.wait()
     mu_copy.wait()
 
@@ -161,12 +178,15 @@
         def _():
             g_copy(step + 1).start()
 
-        for c in range(6):
+        def mix(c):
             g = gv[block, :, c, plane].astype(F32)
             for part in range(2):
                 rows = g[:, part * HALF:(part + 1) * HALF].reshape(depth, WIDE).astype(BF16)
                 both = jnp.dot(mixer[...], rows, preferred_element_type=F32)
                 hbuf[c, part] = both[:size] + both[size:]
+
+        for c in range(5):
+            mix(c)
         start = pl.multiple_of(block * WIDE, WIDE)
         lam = lamv[plane, :, pl.ds(start, WIDE)]
         shear = 2.0 * muv[plane, :, pl.ds(start, WIDE)]
@@ -183,19 +203,41 @@
                 adj[step, source, 2, t] = lam * (h[0] + h[1] + h[2]) + shear * h[2]
                 return 0
 
-            lax.fori_loop(0, snaps, turn, 0, unroll=2)
+            lax.fori_loop(0, snaps, turn, 0, unroll=4)
         to_sibling(step, 1).start()
         to_sibling(step, 0).start()
 
+        def share():
+            to_sibling(step, 1).wait_recv()
+
+            def pass_on(n, _):
+                t = (1 - chip) * quarter + n
+                for k in range(3):
+                    to_par[step, k, n] = (adj[step, core, k, t] + from_sib[step, k, t]).astype(BF16)
+                return 0
+
+            lax.fori_loop(0, quarter, pass_on, 0, unroll=4)
+
+            @pl.when(step < steps - 2)
+            def _():
+                to_partner(step, 0).start()
+
+            @pl.when(step >= steps - 2)
+            def _():
+                to_partner(step, EXTRA).start()
+
+        mix(5)
+
         @pl.when(step == 0)
         def _():
-            send_halo(FIRST, pieces)
+            send_halo(min(FIRST, pieces), pieces)
             at_sides(slab == 0, slab == slabs - 1, blank)
             i, o = iota2(colmat.shape, 0), iota2(colmat.shape, 1)
             colmat[...] = stencil(i - LANES - o).astype(BF16)
             i, o = iota2(rowmat.shape, 1), iota2(rowmat.shape, 0)
             rowmat[...] = jnp.where((i >> 4) == (o >> 4), stencil(i - o), 0.0).astype(BF16)
             edge = jnp.zeros(uv.shape[:-1] + (LANES,), BF16)
+            share()
             u_copy.wait()
             uv[:, :, :, :, :LANES] = edge
             uv[:, :, :, :, LANES + cols:] = edge
@@ -209,16 +251,9 @@
                 dyb[k, part * half * ROW:(part + 1) * half * ROW] = jnp.dot(
                     rowmat[...], rows, preferred_element_type=F32)
 
-        to_sibling(step, 1).wait_recv()
-
-        def pass_on(n, _):
-            t = (1 - chip) * quarter + n
-            for k in range(3):
-                to_par[step, k, n] = (adj[step, core, k, t] + from_sib[step, k, t]).astype(BF16)
-            return 0
-
-        lax.fori_loop(0, quarter, pass_on, 0, unroll=2)
-        to_partner(step).start()
+        @pl.when(step > 0)
+        def _():
+            share()
 
         for source in range(sources):
             def weigh(t, carry):
@@ -238,27 +273,35 @@
             for side in range(2):
                 kacc[2 * block + side, source, plane] = value[:, side * LANES:(side + 1) * LANES]
 
-    def late(piece):
+    def late(piece, last):
         block, side = piece // 2, piece % 2
         lanes = pl.ds(pl.multiple_of(side * LANES, LANES), LANES)
         here = pl.ds(pl.multiple_of(LANES + piece * LANES, LANES), LANES)
 
-        def add(n, totals):
-            at, t = first_of(rcv) + n, chip * quarter + n
+        def add(totals, at, t, near, n, handed):
             new = list(totals)
             for k in range(3):
                 f0, f1 = (uv[at, k, plane, :, here].astype(F32) for plane in range(2))
-                b0, b1 = (halo[0, piece, n, k, plane].astype(F32) for plane in range(2))
-                a0, a1 = (halo[1, piece, n, k, plane].astype(F32) for plane in range(2))
+                b0, b1 = (near(0)[n, k, plane].astype(F32) for plane in range(2))
+                a0, a1 = (near(1)[n, k, plane].astype(F32) for plane in range(2))
                 slopes = 8.0 * (f1 - b1) - (a0 - b0), 8.0 * (a0 - f0) - (a1 - b1)
                 for plane in range(2):
                     step = 2 * block + plane
-                    whole = (adj[step, core, k, t, :, lanes] + from_sib[step, k, t, :, lanes]
-                             + from_par[step, k, n, :, lanes].astype(F32))
+                    whole = adj[step, core, k, t, :, lanes] + from_sib[step, k, t, :, lanes]
+                    if handed:
+                        whole = whole + from_par[step, k, n, :, lanes].astype(F32)
                     new[plane] = new[plane] + slopes[plane] * whole
             return tuple(new)
 
-        totals = lax.fori_loop(0, quarter, add, tuple(kacc[piece, core, plane] for plane in range(2)), unroll=2)
+        def mine(n, totals, handed=True):
+            return add(totals, first_of(rcv) + n, chip * quarter + n, lambda s: halo.at[s, piece], n, handed)
+
+        totals = tuple(kacc[piece, core, plane] for plane in range(2))
+        if last:
+            for n in range(EXTRA):
+                totals = mine(n, totals, False)
+                totals = add(totals, others_of(rcv) + n, (1 - chip) * quarter + n, lambda s: extra.at[s, side], n, False)
+        totals = lax.fori_loop(EXTRA if last else 0, quarter, mine, totals, unroll=True if last else 2)
         for plane in range(2):
             kacc[piece, core, plane] = totals[plane]
 
@@ -275,20 +318,32 @@
         early(step)
         return 0
 
+    def wait_adjoint(block, skip):
+        for plane in range(2):
+            to_sibling(2 * block + plane, 0).wait_recv()
+            to_partner(2 * block + plane, skip).wait_recv()
+
     def finish(piece, _):
         @pl.when(piece % 2 == 0)
         def _():
-            for plane in range(2):
-                to_sibling(2 * (piece // 2) + plane, 0).wait_recv()
-                to_partner(2 * (piece // 2) + plane).wait_recv()
+            wait_adjoint(piece // 2, 0)
 
         at_sides(has_below, has_above, lambda side: halo_copy(side, piece).wait_recv())
-        late(piece)
+        late(piece, False)
         hand_out(piece)
         return 0
 
     lax.fori_loop(0, steps, compute, 0)
-    lax.fori_loop(0, pieces, finish, 0)
+    lax.fori_loop(0, pieces - 2, finish, 0)
+    wait_adjoint(blocks - 1, EXTRA)
+    for n in range(2):
+        def wait_halo(side):
+            halo_copy(side, pieces - 2 + n).wait_recv()
+            extra_copy(side, n).wait_recv()
+
+        at_sides(has_below, has_above, wait_halo)
+        late(pieces - 2 + n, True)
+        hand_out(pieces - 2 + n)
 
     def all_sent(block, sem):
         pltpu.make_async_remote_copy(
@@ -297,7 +352,9 @@
 
     at_sides(has_above, has_below, lambda side: all_sent(halo.at[side], halo_send.at[side]))
     all_sent(from_sib, sib_send)
-    all_sent(from_par, par_send)
+    at_sides(has_above, has_below, lambda side: all_sent(extra.at[side], extra_send.at[side]))
+    all_sent(from_par.at[pl.ds(0, steps - 2)], par_send.at[0])
+    all_sent(from_par.at[pl.ds(steps - 2, 2), :, pl.ds(EXTRA, quarter - EXTRA)], par_send.at[1])
     all_sent(red, red_send)
     for which in range(3):
         pltpu.make_async_copy(red.at[which], red.at[which], red_recv.at[which]).wait()
@@ -326,6 +383,7 @@
             pltpu.VMEM((planes, rows, cols), F32),
             pltpu.VMEM((planes, rows, cols), F32),
             pltpu.VMEM((2, pieces, quarter, parts, planes, rows, LANES), BF16),
+            pltpu.VMEM((2, 2, EXTRA, parts, planes, rows, LANES), BF16),
             pltpu.VMEM((steps, sources, 3, snaps, rows, WIDE), F32),
             pltpu.VMEM((steps, 3, snaps, rows, WIDE), F32),
             pltpu.VMEM((steps, 3, quarter, rows, WIDE), BF16),
@@ -340,7 +398,8 @@
             pltpu.VMEM((pieces, 4, sources, planes, rows // 4, LANES), F32),
             pltpu.VMEM((3, pieces, sources, planes, rows // 4, LANES), F32),
             dma, dma((steps,)), dma, dma,
-            dma((2,)), dma((2, pieces)), dma, dma((steps, 2)), dma, dma((steps,)), dma, dma((3,)),
+            dma((2,)), dma((2, pieces)), dma((2,)), dma((2, 2)), dma, dma((steps, 2)), dma((2,)), dma((steps,)),
+            dma, dma((3,)),
         ],
         compiler_params=pltpu.CompilerParams(
             collective_id=0, has_side_effects=True, vmem_limit_bytes=60 << 20),

time: 51.8 us -> 50.5 us (0.975)
  Pallas kernels: 50.1 us -> 48.9 us
    pallas_call x1, Pallas kernels: 50.1 us -> 48.9 us  [on_device(): pl.pallas_call(functools.partial(kernel, sources, snaps, stations, lags),...]
where the time goes in v4:
time: 50.5 us; the launch traced here: 50.3 us
  Pallas kernels  48.9 us (97%)
  local copies, waits for them, and re-layouts  1.47 us (3%)
    pallas_call x1, Pallas kernels, on_device(): pl.pallas_call(functools.partial(kernel, sources, snaps, stations, lags),...  48.9 us
    unnamed x1, local copies, waits for them, and re-layouts  1.47 us

profile of v4, /device:TPU:161, one launch (start us, length us, event | category | flops | bytes accessed | tf_op | source)
XLA Modules:
  0.0 50.3 jit_solution(10275487849641899841)
XLA Ops:
  0.0 48.9 %shard_map.64 = f32[2,2,4,1024]{3,2,1,0:T(4,128)} custom-call(bf16[32,3,2,16,1024]{4,3,2,1,0:T(8,128)(2,1)} %bitcast.3, bf16[32,6,2,16,1024]{4,3,2,1,0:T(8,128)(2,1)} %bitcast.2, f32[2,16,1024]{2,1,0:T(8,128)} %lam_hbm.1, f32[2,16,1024]{2,1,0:T(8,128)} %mu_hbm.1, f32[2,2,9]{2,1,0:T(2,128)} %filt.1, s32[2,2]{1,0:T(2,128)} %pairs.1), custom_call_target="tpu_custom_call" | custom-call | flops 25999998976 | bytes 20000000 | tf_op jit(solution)/shard_map/pallas_call | solution.py:375
  48.9 1.5 %copy.8 = f32[2,2,4,1024]{3,2,1,0:T(4,128)} copy(f32[2,2,4,1024]{3,2,1,0:T(4,128)} %shard_map.64) | data formatting | bytes 131072

commit v5 on v4

--- a/solution.py
+++ b/solution.py
@@ -143,8 +143,6 @@
         mixer[n * size:(n + 1) * size] = jnp.where(
             same_row, jnp.dot(tall, spread_t, preferred_element_type=F32), 0.0).astype(BF16)
 
-    pl.semaphore_wait(barrier, 3 + count_above + count_below)
-
     def send_halo(first, last):
         def send(side):
             for piece in range(first, last):
@@ -159,7 +157,6 @@
         halo[side] = jnp.zeros(halo.shape[1:], BF16)
         extra[side] = jnp.zeros(extra.shape[1:], BF16)
 
-    send_halo(0, min(FIRST, pieces))
     lam_copy.wait()
     mu_copy.wait()
 
@@ -204,6 +201,12 @@
                 return 0
 
             lax.fori_loop(0, snaps, turn, 0, unroll=4)
+
+        @pl.when(step == 0)
+        def _():
+            pl.semaphore_wait(barrier, 3 + count_above + count_below)
+            send_halo(0, min(FIRST, pieces))
+
         to_sibling(step, 1).start()
         to_sibling(step, 0).start()
 

time: 50.5 us -> 50.1 us (level)
  Pallas kernels: 48.9 us -> 48.1 us
    pallas_call x1, Pallas kernels: 48.9 us -> 48.1 us  [on_device(): pl.pallas_call(functools.partial(kernel, sources, snaps, stations, lags),...]
where the time goes in v5:
time: 50.1 us; the launch traced here: 49.6 us
  Pallas kernels  48.1 us (96%)
  local copies, waits for them, and re-layouts  1.47 us (3%)
    pallas_call x1, Pallas kernels, on_device(): pl.pallas_call(functools.partial(kernel, sources, snaps, stations, lags),...  48.1 us
    unnamed x1, local copies, waits for them, and re-layouts  1.47 us

profile of v5, /device:TPU:161, one launch (start us, length us, event | category | flops | bytes accessed | tf_op | source)
XLA Modules:
  0.0 49.6 jit_solution(10086472705041299375)
XLA Ops:
  0.0 48.1 %shard_map.64 = f32[2,2,4,1024]{3,2,1,0:T(4,128)} custom-call(bf16[32,3,2,16,1024]{4,3,2,1,0:T(8,128)(2,1)} %bitcast.3, bf16[32,6,2,16,1024]{4,3,2,1,0:T(8,128)(2,1)} %bitcast.2, f32[2,16,1024]{2,1,0:T(8,128)} %lam_hbm.1, f32[2,16,1024]{2,1,0:T(8,128)} %mu_hbm.1, f32[2,2,9]{2,1,0:T(2,128)} %filt.1, s32[2,2]{1,0:T(2,128)} %pairs.1), custom_call_target="tpu_custom_call" | custom-call | flops 25999998976 | bytes 20000000 | tf_op jit(solution)/shard_map/pallas_call | solution.py:378
  48.2 1.5 %copy.8 = f32[2,2,4,1024]{3,2,1,0:T(4,128)} copy(f32[2,2,4,1024]{3,2,1,0:T(4,128)} %shard_map.64) | data formatting | bytes 131072
